TPU v7x, 32 devices: a whole 2x2x4 slice. The times are simulated.
32 devices in a mesh: lat: 8 (over y, x, core), lev: 4 (over z).
Axes of the slice: x: 2, y: 2, z: 4, core: 2. Of those that a mesh axis runs over, the one named last changes fastest.
Arguments:
- tracer: float32 [8, 640, 1280], P('lev', 'lat'), may hold values from -6 to 6
- offsets: int32 [2, 640, 1280], P(None, 'lat'), may hold values from -3 to 3
- stencil: float32 [7, 7], replicated, may hold values from -0.6 to 0.6
- assign: int32 [640], replicated, may hold values from 0 to 639, as said below
- legendre: bfloat16 [640, 2, 320, 320], P('lat', None, 'lev'), may hold values from -0.3125 to 0.3125
- damping: float32 [8], replicated, may hold values from 0.5 to 8
- vert_vecs: float32 [8, 8], replicated, may hold values from -2 to 2
- vert_inv: float32 [8, 8], replicated, may hold values from -2 to 2
Outputs:
- tracer_new: float32 [8, 640, 1280], P('lev', 'lat')
- spectral_new: float32 [640, 2, 320, 16], P('lat', None, 'lev')
Inputs may be any that keep to these rules, and one draw needn't show every extreme that they name: `assign`: a permutation of 0 to 639 in which slots 2 u and 2 u + 1 hold the wavenumbers m and 639 - m.
All inputs are finite; a program needn't handle non-finite values.
Results may differ from a plain program's by a relative error of at most 0.0036.
Values may be sent and summed in bfloat16 or wider, within the bound.
A program may use at most 192 MiB of HBM per device.

v0:
```python
import math
import jax
import jax.numpy as jnp
from jax import lax
from jax.sharding import PartitionSpec as P

M = 640
EXACT = lax.Precision.HIGHEST


def padded_2(cells, sides, width):
    for axis, dim in sides:
        count = lax.axis_size(axis)
        ends = count - 1
        head = lax.slice_in_dim(cells, 0, width, axis=dim)
        tail = lax.slice_in_dim(cells, cells.shape[dim] - width, cells.shape[dim], axis=dim)
        cells = jnp.concatenate(
            [
                lax.ppermute(tail, axis, [(i, (i + 1) % count) for i in range(ends)]),
                cells,
                lax.ppermute(head, axis, [((i + 1) % count, i) for i in range(ends)]),
            ],
            axis=dim,
        )
    return cells


def transport(padded, offsets, stencil):
    row_count = offsets.shape[1]
    summed = jnp.zeros((padded.shape[0], row_count, padded.shape[2]), jnp.float32)
    for row_step in range(-3, 4):
        band_rows = padded[:, 3 + row_step : 3 + row_step + row_count, :]
        for col_step in range(-3, 4):
            shifted = jnp.roll(band_rows, -col_step, axis=2)
            picked = jnp.logical_and(offsets[0] == row_step, offsets[1] == col_step).astype(
                jnp.float32
            )
            summed = summed + (stencil[row_step + 3, col_step + 3] + picked)[None, :, :] * shifted
    return summed


def wave_angles(assign, lon_cells):
    longitudes = jnp.arange(lon_cells, dtype=jnp.int32)
    phase_index = longitudes[:, None] * assign[None, :] % lon_cells
    angles = phase_index.astype(jnp.float32) * (2.0 * math.pi / lon_cells)
    return (angles, 1.0 / math.sqrt(lon_cells))


def forward_table(assign, lon_cells):
    angles, norm_scale = wave_angles(assign, lon_cells)
    return jnp.stack([jnp.cos(angles) * norm_scale, -jnp.sin(angles) * norm_scale], axis=2)


def inverse_table(assign, lon_cells):
    angles, norm_scale = wave_angles(assign, lon_cells)
    weights = jnp.where(assign == 0, 1.0, 2.0).astype(jnp.float32) * norm_scale
    cosines = jnp.cos(angles).T * weights[:, None]
    sines = -jnp.sin(angles).T * weights[:, None]
    return jnp.stack([cosines, sines], axis=1)


def split_hemispheres(fourier):
    half_lat = fourier.shape[-1] // 2
    north_half = fourier[..., :half_lat]
    south_half = fourier[..., ::-1][..., :half_lat]
    return jnp.stack([north_half + south_half, north_half - south_half], axis=1).astype(
        jnp.bfloat16
    )


def vertical(spectra, my_waves, first_degree, damping, vert_vecs, vert_inv):
    degree_span = spectra.shape[2]
    degrees = first_degree + jnp.arange(degree_span, dtype=jnp.int32)
    parity = jnp.arange(2, dtype=jnp.int32)
    degree_n = my_waves[:, None, None] + 2 * degrees[None, None, :] + parity[None, :, None]
    inside = (degree_n <= M - 1).astype(jnp.float32)
    forcing = spectra * inside[:, :, :, None, None]
    modal = jnp.einsum("kq,rpicq->rpick", vert_inv, forcing, precision=EXACT)
    scaled_n = degree_n.astype(jnp.float32)
    growth = scaled_n * (scaled_n + 1.0) / float(M * M)
    denominator = 1.0 + growth[:, :, :, None, None] * damping[None, None, None, None, :]
    modal = modal / denominator
    return jnp.einsum("kq,rpicq->rpick", vert_vecs, modal, precision=EXACT)


def on_device(tracer, offsets, stencil, assign, legendre, damping, vert_vecs, vert_inv):
    lon_cells = tracer.shape[2]
    padded = padded_2(tracer, (("lat", 1),), 3)
    advected = transport(padded, offsets, stencil)
    fourier = jnp.einsum(
        "lij,jrc->rcli", advected, forward_table(assign, lon_cells), precision=EXACT
    )
    by_wave = lax.all_to_all(fourier, "lat", split_axis=0, concat_axis=3, tiled=True)
    hemispheres = split_hemispheres(by_wave)
    slot_count = legendre.shape[0]
    my_waves = lax.dynamic_slice_in_dim(assign, lax.axis_index("lat") * slot_count, slot_count)
    first_degree = lax.axis_index("lev") * legendre.shape[2]
    full_table = lax.all_gather(legendre, "lev", axis=2, tiled=True)
    spectra_all = jnp.einsum(
        "rpij,rpclj->rpicl", full_table, hemispheres, preferred_element_type=jnp.float32
    )
    spectra = lax.all_to_all(spectra_all, "lev", split_axis=2, concat_axis=4, tiled=True)
    solved = vertical(spectra, my_waves, first_degree, damping, vert_vecs, vert_inv)
    packed = solved.astype(jnp.bfloat16)
    spread = lax.all_to_all(packed, "lev", split_axis=4, concat_axis=2, tiled=True)
    back_terms = jnp.einsum(
        "rpij,rpicl->lrpcj", full_table, spread, preferred_element_type=jnp.float32
    )
    north_half = back_terms[:, :, 0] + back_terms[:, :, 1]
    south_half = back_terms[:, :, 0] - back_terms[:, :, 1]
    zonal = jnp.concatenate([north_half, south_half[..., ::-1]], axis=-1)
    lat_rows = lax.all_to_all(zonal, "lat", split_axis=3, concat_axis=1, tiled=True)
    tracer_new = jnp.einsum(
        "lrci,rcj->lij", lat_rows, inverse_table(assign, lon_cells), precision=EXACT
    )
    spectral_new = solved.reshape(solved.shape[0], 2, solved.shape[2], 2 * solved.shape[4])
    return (tracer_new, spectral_new)


def solution(mesh):
    in_specs = (
        P("lev", "lat", None),
        P(None, "lat", None),
        P(),
        P(),
        P("lat", None, "lev", None),
        P(),
        P(),
        P(),
    )
    out_specs = (P("lev", "lat", None), P("lat", None, "lev", None))
    return jax.shard_map(
        on_device, mesh=mesh, in_specs=in_specs, out_specs=out_specs, check_vma=False
    )
```

profile of v0, /device:TPU:0, one launch (start us, length us, event | category | flops | bytes accessed | tf_op | source)
XLA Modules:
  0.0 811.9 jit_solution(14464015490012806624)
XLA Ops:
  8.4 2.4 collective-permute-start
  10.8 1.3 collective-permute-start.1
  14.2 1.5 add_bitcast_fusion.48
  15.8 5.6 add_bitcast_fusion.41
  21.4 5.5 add_bitcast_fusion.47
  26.9 1.5 add_bitcast_fusion.21
  28.3 9.1 %add_bitcast_fusion.26 = (f32[80,1280]{1,0:T(8,128)}, f32[80,1280]{1,0:T(8,128)}, f32[80,1280]{1,0:T(8,128)}, f32[80,1280]{1,0:T(8,128)}, f32[80,1280]{1,0:T(8,1...) fusion(pred[1,80,1280]{2,1,0:T(8,128)(4,1)S(1)} %get-tuple-elem, ...), kind=kLoop, calls=%fused_computation.329 | loop fusion | flops 3379200 | bytes 5324844 | tf_op jit(solution)/shard_map/mul | solution.py:38
  37.4 9.3 %add_bitcast_fusion.40 = (f32[80,1280]{1,0:T(8,128)S(1)}, f32[80,1280]{1,0:T(8,128)S(1)}, f32[80,1280]{1,0:T(8,128)S(1)}, f32[80,1280]{1,0:T(8,128)S(1)}, f32[80...) fusion(pred[1,80,1280]{2,1,0:T(8,128)(4,1)S(1)} %get-tuple-elem, ...), kind=kLoop, calls=%fused_computation.357 | loop fusion | flops 3686400 | bytes 5632048 | tf_op jit(solution)/shard_map/mul | solution.py:38
  46.6 9.6 %add_bitcast_fusion.38 = (f32[80,1280]{1,0:T(8,128)}, f32[80,1280]{1,0:T(8,128)}, f32[80,1280]{1,0:T(8,128)}, f32[80,1280]{1,0:T(8,128)}, f32[80,1280]{1,0:T(8,1...) fusion(pred[1,80,1280]{2,1,0:T(8,128)(4,1)S(1)} %get-tuple-elem, ...), kind=kLoop, calls=%fused_computation.353 | loop fusion | flops 3686400 | bytes 5632048 | tf_op jit(solution)/shard_map/mul | solution.py:38
  56.2 23.1 %cosine_multiply_fusion.1 = (f32[1280,640,1]{1,0,2:T(8,128)S(1)}, f32[1280,640,1]{1,0,2:T(8,128)S(1)}) fusion(s32[640]{0:T(1024)S(1)} %copy-done.5), kind=kLoop, calls=%fused_computation.62 | loop fusion | flops 9830400 | bytes 6556160 | tf_op jit(solution)/shard_map/mul | solution.py:51
  79.4 0.9 fusion.232
  80.3 0.9 fusion.234
  81.2 0.9 fusion.236
  82.1 0.8 fusion.219
  82.9 1.0 fusion.215
  83.9 1.0 fusion.222
  84.8 2.9 fusion.231
  87.8 2.9 fusion.233
  90.7 3.0 fusion.235
  93.7 3.8 fusion.72
  97.5 3.8 fusion.73
  101.3 3.7 fusion.237
  105.0 28.9 %fusion.4 = f32[640,2,2,80]{0,3,2,1:T(8,128)S(1)} fusion(f32[1280,640,1]{1,0,2:T(8,128)S(1)} %get-tuple-element.229, f32[1280,640,1]{1,0,2:T(8,128)S(1)} %get-tuple-element.228, f32[2,83,1280]{2,1,0:T(8,128)S(1)} %constant_dynamic-update-slice_fusion, f32[2,80,1]{2,1,0:T(8,128)} %get-tuple-element.138, f32[2,80,1279]{2,1,0:T(8,128)} %get-tuple-element.137, ...), kind=kOutput, calls=%fused_computation.43 | convolution fusion | flops 3176652800 | bytes 65405440 | tf_op jit(solution)/shard_map/lij,jrc->rcli/dot_general | solution.py:90
  133.9 0.9 copy.54
  134.8 25.3 %all_to_all.72 = f32[640,2,2,80]{3,2,1,0:T(2,128)S(1)} all-to-all(f32[640,2,2,80]{3,2,1,0:T(2,128)S(1)} %copy.54), channel_id=1, replica_groups=mesh['lat'=8,'lev'=4] {'lat'}, dimensions={0} | all-to-all | bytes 1638400 | tf_op jit(solution)/shard_map/all_to_all | solution.py:93
  160.2 0.8 copy.82
  160.9 1.1 all_to_all.55
  162.6 1.5 reverse.1
  164.9 504.5 %all-gather.2.cloned.1.call-done = bf16[80,2,320,320]{3,2,1,0:T(8,128)(2,1)} async-done(((bf16[80,2,80,320]{3,2,1,0:T(8,128)(2,1)}), bf16[80,2,320,320]{3,2,1,0:T(8,128)(2,1)}) %all-gather.2.cloned.1.call-update) | async-done | bytes 32768016 | tf_op jit(solution)/shard_map/all_gather | solution.py:98
  669.5 17.4 %fusion.21 = f32[80,2,320,2,2]{2,4,3,1,0:T(2,128)S(1)} fusion(bf16[80,2,320,320]{3,2,1,0:T(8,128)(2,1)} %all-gather.2.cloned.1.call-done, bf16[80,1,2,2,320]{4,3,2,1,0:T(2,128)(2,1)S(1)} %fusion.204, bf16[80,1,2,2,320]{4,3,2,1,0:T(2,128)(2,1)S(1)} %get-tuple-element.2), kind=kOutput, calls=%fused_computation.70 | convolution fusion | flops 131891200 | bytes 33996800 | tf_op jit(solution)/shard_map/rpij,rpclj->rpicl/dot_general | solution.py:99
  686.9 2.0 copy.57
  689.0 3.5 all-to-all-start.1
  692.8 1.0 multiply_add_fusion
  693.7 30.4 %all-to-all-done.1 = f32[80,2,320,2,2]{0,4,3,1,2:T(2,128)S(1)} async-done(((f32[80,2,320,2,2]{0,4,3,1,2:T(2,128)}), f32[80,2,320,2,2]{0,4,3,1,2:T(2,128)S(1)}, u32[]{:S(2)}, u32[]{:S(2)}) %all-to-all-start.1) | async-done | bytes 819232 | tf_op jit(solution)/shard_map/all_to_all | solution.py:102
  724.1 1.2 copy.74
  725.6 0.8 copy-done.3
  726.4 1.6 convolution_divide_fusion
  728.0 2.3 fusion.242
  730.8 19.7 %all_to_all.73 = bf16[80,2,80,2,8]{2,3,1,0,4:T(2,128)(2,1)S(1)} all-to-all(bf16[80,2,80,2,8]{2,3,1,0,4:T(2,128)(2,1)S(1)} %copy.62), channel_id=1, replica_groups=mesh['lat'=8,'lev'=4] {'lev'}, dimensions={4} | all-to-all | bytes 819200 | tf_op jit(solution)/shard_map/all_to_all | solution.py:105
  750.5 0.8 copy.83
  751.3 1.3 all_to_all.63
  752.6 15.5 %fusion.24 = f32[2,80,2,2,320]{4,0,3,2,1:T(2,128)S(1)} fusion(bf16[80,2,320,2,2]{2,4,3,1,0:T(2,128)(2,1)S(1)} %all_to_all.63, bf16[80,2,320,320]{3,2,1,0:T(8,128)(2,1)} %all-gather.2.cloned.1.call-done), kind=kOutput, calls=%fused_computation.71 | convolution fusion | flops 131072000 | bytes 33996800 | tf_op jit(solution)/shard_map/rpij,rpicl->lrpcj/dot_general | solution.py:106
  768.6 1.5 reverse.2
  771.3 2.7 copy.67
  774.1 3.8 all-to-all-start.3
  777.9 16.0 %cosine_multiply_fusion = (f32[640,1,1280]{2,0,1:T(8,128)}, f32[640,1,1280]{2,0,1:T(8,128)}) fusion(f32[640]{0:T(1024)S(1)} %select_multiply_fusion, s32[640]{0:T(1024)S(1)} %copy-done.5), kind=kLoop, calls=%fused_computation.57 | loop fusion | flops 9830400 | bytes 6558720 | tf_op jit(solution)/shard_map/mul | solution.py:57
  793.9 2.1 all-to-all-done.3
  797.2 7.7 fusion.20
  (44 shorter events, 8.6 us)
Async XLA Ops:
  7.2 720.9 %copy-start = (f32[8,8]{1,0:T(8,128)S(1)}, f32[8,8]{1,0:T(8,128)}, u32[]{:S(2)}) copy-start(f32[8,8]{1,0:T(8,128)} %param.14) | copy-start | bytes 772
  7.2 1.2 copy-start.1
  7.2 4.9 copy-start.4
  7.2 7.0 copy-start.2
  7.2 662.3 %all-gather.2.cloned.1.call-start = ((), (), s32[]{:S(2)}) async-start(), calls=%async_computation.4 | async-start | bytes 49152000 | tf_op jit(solution)/shard_map/all_gather | solution.py:98
  8.4 73.7 %collective-permute-start = (f32[2,3,1280]{2,1,0:T(4,128)S(1)}, f32[2,3,1280]{2,1,0:T(4,128)S(1)}, u32[]{:S(2)}, u32[]{:S(2)}) collective-permute-start(f32[2,3,1280]{2,1,0:T(4,128)S(1)} %get-tuple-element.140), channel_id=1, source_target_pairs={{0,4},{4,8},{8,12},{12,16},{16,20},{20,24},{24,28},{1,5},{5,9},{9,... | collective-permute-start | bytes 92168 | tf_op jit(solution)/shard_map/ppermute | solution.py:19
  10.8 68.7 %collective-permute-start.1 = (f32[2,3,1280]{2,1,0:T(4,128)S(1)}, f32[2,3,1280]{2,1,0:T(4,128)S(1)}, u32[]{:S(2)}, u32[]{:S(2)}) collective-permute-start(f32[2,3,1280]{2,1,0:T(4,128)S(1)} %get-tuple-element.141), channel_id=1, source_target_pairs={{4,0},{8,4},{12,8},{16,12},{20,16},{24,20},{28,24},{5,1},{9,5},{13... | collective-permute-start | bytes 92168 | tf_op jit(solution)/shard_map/ppermute | solution.py:21
  46.6 9.6 %copy-start.5 = (s32[640]{0:T(1024)S(1)}, s32[640]{0:T(1024)}, u32[]{:S(2)}) copy-start(s32[640]{0:T(1024)} %param.11) | copy-start | bytes 7684
  686.9 5.9 copy-start.6
  689.0 35.2 %all-to-all-start.1 = ((f32[80,2,320,2,2]{0,4,3,1,2:T(2,128)}), f32[80,2,320,2,2]{0,4,3,1,2:T(2,128)S(1)}, u32[]{:S(2)}, u32[]{:S(2)}) async-start(f32[80,2,320,2,2]{0,4,3,1,2:T(2,128)} %copy.57), calls=%async_computation.1 | async-start | bytes 2621440 | tf_op jit(solution)/shard_map/all_to_all | solution.py:102
  725.3 1.1 copy-start.3
  725.3 1.1 copy-start.7
  774.1 21.9 %all-to-all-start.3 = ((f32[2,80,2,640]{1,2,0,3:T(2,128)}), f32[2,80,2,640]{1,2,0,3:T(2,128)S(1)}, u32[]{:S(2)}, u32[]{:S(2)}) async-start(f32[2,80,2,640]{1,2,0,3:T(2,128)} %copy.67), calls=%async_computation.3 | async-start | bytes 2621440 | tf_op jit(solution)/shard_map/all_to_all | solution.py:112
Sparse Core Ops, SparseCore 0:
  9.6 659.8 all-gather.1
where the time goes:
time: 821 us; the launch traced here: 812 us
  waiting for transfers between devices  538 us (66%)
  other arithmetic  98.4 us (12%)
  matrix products  73.4 us (9%)
  blocking collectives  45 us (5%)
  local copies, waits for them, and re-layouts  31.8 us (4%)
  between operations  14.6 us (2%)
  starting transfers between devices  11.1 us (1%)
    all_gather x1, waiting for transfers between devices, on_device(): full_table = lax.all_gather(legendre, 'lev', axis=2, tiled=True)  505 us
    mul x7, other arithmetic, transport(): (stencil[row_step + 3, col_step + 3] + picked)[None, :, :] * shifted  42 us
    all_to_all x1, waiting for transfers between devices, on_device(): lax.all_to_all(spectra_all, 'lev', split_axis=2, concat_axis=4, tiled=True)  30.4 us
    dot_general x1, matrix products, on_device(): jnp.einsum('lij,jrc->rcli', advected, forward_table(assign, lon_cells), p...  28.9 us
    all_to_all x1, blocking collectives, on_device(): lax.all_to_all(fourier, 'lat', split_axis=0, concat_axis=3, tiled=True)  25.3 us
    mul x1, other arithmetic, forward_table(): jnp.cos(angles) * norm_scale  23.1 us
    all_to_all x1, blocking collectives, on_device(): lax.all_to_all(packed, 'lev', split_axis=4, concat_axis=2, tiled=True)  19.7 us
    dot_general x1, matrix products, on_device(): jnp.einsum('rpij,rpclj->rpicl', full_table, hemispheres, preferred_elemen...  17.4 us
  transfers between devices with their start and end apart: 5, of which 3 were waited for; matrix products, arithmetic and copies ran while one was open for 18% of the time, Pallas kernels for 0%

commit v1 on v0

--- a/solution.py
+++ b/solution.py
@@ -95,7 +95,13 @@
     slot_count = legendre.shape[0]
     my_waves = lax.dynamic_slice_in_dim(assign, lax.axis_index("lat") * slot_count, slot_count)
     first_degree = lax.axis_index("lev") * legendre.shape[2]
-    full_table = lax.all_gather(legendre, "lev", axis=2, tiled=True)
+    peers = lax.axis_size("lev")
+    held, blocks = (legendre, [legendre])
+    for _ in range(peers - 1):
+        held = lax.ppermute(held, "lev", [(i_2, (i_2 + 1) % peers) for i_2 in range(peers)])
+        blocks.insert(0, held)
+    line = jnp.concatenate(blocks, axis=2)
+    full_table = jnp.roll(line, (lax.axis_index("lev") + 1) * legendre.shape[2], axis=2)
     spectra_all = jnp.einsum(
         "rpij,rpclj->rpicl", full_table, hemispheres, preferred_element_type=jnp.float32
     )

time: 821 us -> 859 us (1.046)
  local copies, waits for them, and re-layouts: 31.8 us -> 105 us
  blocking collectives: 45 us -> 19.5 us
  between operations: 14.6 us -> 1.52 us
    all_gather x1 -> x0, waiting for transfers between devices: 505 us -> none  [on_device(): full_table = lax.all_gather(legendre, 'lev', axis=2, tiled=True)]
    ppermute x0 -> x3, waiting for transfers between devices: none -> 490 us  [on_device(): lax.ppermute(held, 'lev', [(i_2, (i_2 + 1) % peers) for i_2 in range(peer...]
    unnamed x20 -> x27, local copies, waits for them, and re-layouts: 4.81 us -> 64.1 us
    all_to_all x1 -> x0, blocking collectives: 25.3 us -> none  [on_device(): lax.all_to_all(fourier, 'lat', split_axis=0, concat_axis=3, tiled=True)]
    all_to_all x0 -> x1, waiting for transfers between devices: none -> 18.1 us  [on_device(): lax.all_to_all(fourier, 'lat', split_axis=0, concat_axis=3, tiled=True)]
    mul x1, other arithmetic: 23.1 us -> 13.4 us  [forward_table(): jnp.cos(angles) * norm_scale]
  transfers between devices with their start and end apart: 5 -> 8, of which waited for: 3 -> 6; matrix products, arithmetic and copies ran while one was open for 18% -> 17% of each run, Pallas kernels for 0% -> 0%
where the time goes in v1:
time: 859 us; the launch traced here: 849 us
  waiting for transfers between devices  538 us (63%)
  local copies, waits for them, and re-layouts  105 us (12%)
  other arithmetic  90.7 us (11%)
  matrix products  74.5 us (9%)
  blocking collectives  19.5 us (2%)
  starting transfers between devices  18.9 us (2%)
    ppermute x3, waiting for transfers between devices, on_device(): lax.ppermute(held, 'lev', [(i_2, (i_2 + 1) % peers) for i_2 in range(peer...  490 us
    unnamed x27, local copies, waits for them, and re-layouts  64.1 us
    mul x7, other arithmetic, transport(): (stencil[row_step + 3, col_step + 3] + picked)[None, :, :] * shifted  44 us
    dot_general x1, matrix products, on_device(): jnp.einsum('lij,jrc->rcli', advected, forward_table(assign, lon_cells), p...  28.9 us
    all_to_all x1, waiting for transfers between devices, on_device(): lax.all_to_all(spectra_all, 'lev', split_axis=2, concat_axis=4, tiled=True)  28.1 us
    all_to_all x1, blocking collectives, on_device(): lax.all_to_all(packed, 'lev', split_axis=4, concat_axis=2, tiled=True)  19.5 us
    all_to_all x1, waiting for transfers between devices, on_device(): lax.all_to_all(fourier, 'lat', split_axis=0, concat_axis=3, tiled=True)  18.1 us
    dot_general x1, matrix products, on_device(): jnp.einsum('rpij,rpclj->rpicl', full_table, hemispheres, preferred_elemen...  17.4 us
  transfers between devices with their start and end apart: 8, of which 6 were waited for; matrix products, arithmetic and copies ran while one was open for 17% of the time, Pallas kernels for 0%

profile of v1, /device:TPU:0, one launch (start us, length us, event | category | flops | bytes accessed | tf_op | source)
XLA Modules:
  0.0 848.7 jit_solution(1253650065297277753)
XLA Ops:
  0.7 3.1 collective-permute-start
  3.8 213.6 %collective-permute-done = bf16[80,2,80,320]{3,2,1,0:T(8,128)(2,1)S(1)} collective-permute-done((bf16[80,2,80,320]{3,2,1,0:T(8,128)(2,1)}, bf16[80,2,80,320]{3,2,1,0:T(8,128)(2,1)S(1)}, u32[]{:S(2)}, u32[]{:S(2)}) %collective-permute-start) | collective-permute-done | bytes 8192032 | tf_op jit(solution)/shard_map/ppermute | solution.py:101
  219.8 3.0 collective-permute-start.3
  222.8 1.8 fusion.242
  224.6 2.1 fusion.241
  226.7 2.1 fusion.240
  228.8 2.7 add_bitcast_fusion.48
  231.5 6.5 add_bitcast_fusion.41
  238.0 5.5 add_bitcast_fusion.47
  243.4 1.5 add_bitcast_fusion.21
  245.0 8.8 %add_bitcast_fusion.26 = (f32[80,1280]{1,0:T(8,128)}, f32[80,1280]{1,0:T(8,128)}, f32[80,1280]{1,0:T(8,128)}, f32[80,1280]{1,0:T(8,128)}, f32[80,1280]{1,0:T(8,1...) fusion(pred[1,80,1280]{2,1,0:T(8,128)(4,1)S(1)} %get-tuple-elem, ...), kind=kLoop, calls=%fused_computation.330 | loop fusion | flops 3379200 | bytes 5324844 | tf_op jit(solution)/shard_map/mul | solution.py:38
  253.8 9.4 %add_bitcast_fusion.38 = (f32[80,1280]{1,0:T(8,128)S(1)}, f32[80,1280]{1,0:T(8,128)S(1)}, f32[80,1280]{1,0:T(8,128)S(1)}, f32[80,1280]{1,0:T(8,128)S(1)}, f32[80...) fusion(pred[1,80,1280]{2,1,0:T(8,128)(4,1)S(1)} %get-tuple-elem, ...), kind=kLoop, calls=%fused_computation.354 | loop fusion | flops 3686400 | bytes 5632048 | tf_op jit(solution)/shard_map/mul | solution.py:38
  263.2 9.7 %add_bitcast_fusion.40 = (f32[80,1280]{1,0:T(8,128)}, f32[80,1280]{1,0:T(8,128)}, f32[80,1280]{1,0:T(8,128)}, f32[80,1280]{1,0:T(8,128)}, f32[80,1280]{1,0:T(8,1...) fusion(pred[1,80,1280]{2,1,0:T(8,128)(4,1)S(1)} %get-tuple-elem, ...), kind=kLoop, calls=%fused_computation.358 | loop fusion | flops 3686400 | bytes 5632048 | tf_op jit(solution)/shard_map/mul | solution.py:38
  272.9 13.4 %cosine_multiply_fusion.1 = (f32[1280,640,1]{1,0,2:T(8,128)S(1)}, f32[1280,640,1]{1,0,2:T(8,128)S(1)}) fusion(s32[640]{0:T(1024)S(1)} %copy-done.5), kind=kLoop, calls=%fused_computation.64 | loop fusion | flops 9830400 | bytes 6556160 | tf_op jit(solution)/shard_map/mul | solution.py:51
  289.0 142.8 %collective-permute-done.1 = bf16[80,2,80,320]{3,2,1,0:T(8,128)(2,1)} collective-permute-done((bf16[80,2,80,320]{3,2,1,0:T(8,128)(2,1)S(1)}, bf16[80,2,80,320]{3,2,1,0:T(8,128)(2,1)}, u32[]{:S(2)}, u32[]{:S(2)}) %collective-permute-start.1) | collective-permute-done | bytes 8192032 | tf_op jit(solution)/shard_map/ppermute | solution.py:101
  434.9 3.0 fusion.232
  437.9 3.0 fusion.234
  440.9 2.9 fusion.236
  443.8 3.8 fusion.71
  447.6 3.7 fusion.72
  451.4 3.7 fusion.238
  455.1 28.9 %fusion.6 = f32[640,2,2,80]{0,3,2,1:T(8,128)S(1)} fusion(f32[1280,640,1]{1,0,2:T(8,128)S(1)} %get-tuple-element.229, f32[1280,640,1]{1,0,2:T(8,128)S(1)} %get-tuple-element.228, f32[2,83,1280]{2,1,0:T(8,128)S(1)} %constant_dynamic-update-slice_fusion.8, f32[2,80,1]{2,1,0:T(8,128)} %get-tuple-element.138, f32[2,80,1279]{2,1,0:T(8,128)} %get-tuple-element.137, ...), kind=kOutput, calls=%fused_computation.45 | convolution fusion | flops 3176652800 | bytes 65405440 | tf_op jit(solution)/shard_map/lij,jrc->rcli/dot_general | solution.py:90
  485.4 3.7 all-to-all-start
  489.2 18.1 %all-to-all-done = f32[640,2,2,80]{3,2,1,0:T(2,128)S(1)} async-done(((f32[640,2,2,80]{3,2,1,0:T(2,128)}), f32[640,2,2,80]{3,2,1,0:T(2,128)S(1)}, u32[]{:S(2)}, u32[]{:S(2)}) %all-to-all-start) | async-done | bytes 819232 | tf_op jit(solution)/shard_map/all_to_all | solution.py:93
  509.7 1.5 reverse.1
  512.0 133.9 %collective-permute-done.2 = bf16[80,2,80,320]{3,2,1,0:T(8,128)(2,1)} collective-permute-done((bf16[80,2,80,320]{3,2,1,0:T(8,128)(2,1)}, bf16[80,2,80,320]{3,2,1,0:T(8,128)(2,1)}, u32[]{:S(2)}, u32[]{:S(2)}) %collective-permute-start.2) | collective-permute-done | bytes 8192032 | tf_op jit(solution)/shard_map/ppermute | solution.py:101
  645.9 8.5 %constant_dynamic-update-slice_fusion.7 = bf16[80,2,640,320]{3,2,1,0:T(8,128)(2,1)} fusion(bf16[80,2,80,320]{3,2,1,0:T(8,128)(2,1)} %collective-permute-done.2), kind=kLoop, calls=%fused_computation.420 | loop fusion | bytes 18022400
  654.4 8.6 %constant_dynamic-update-slice_fusion.6 = bf16[80,2,640,320]{3,2,1,0:T(8,128)(2,1)} fusion(bf16[80,2,640,320]{3,2,1,0:T(8,128)(2,1)} %constant_dynamic-update-slice_fusion.7, bf16[80,2,80,320]{3,2,1,0:T(8,128)(2,1)} %collective-permute-done.1), kind=kLoop, calls=%fused_computation.419 | loop fusion | bytes 19660800
  663.0 8.5 %constant_dynamic-update-slice_fusion.5 = bf16[80,2,640,320]{3,2,1,0:T(8,128)(2,1)} fusion(bf16[80,2,640,320]{3,2,1,0:T(8,128)(2,1)} %constant_dynamic-update-slice_fusion.6, bf16[80,2,80,320]{3,2,1,0:T(8,128)(2,1)} %copy-done.2), kind=kLoop, calls=%fused_computation.418 | loop fusion | bytes 19660800
  671.6 8.5 constant_dynamic-update-slice_fusion.4
  680.0 8.5 constant_dynamic-update-slice_fusion.3
  688.5 8.6 %constant_dynamic-update-slice_fusion.2 = bf16[80,2,640,320]{3,2,1,0:T(8,128)(2,1)} fusion(bf16[80,2,640,320]{3,2,1,0:T(8,128)(2,1)} %constant_dynamic-update-slice_fusion.3, bf16[80,2,80,320]{3,2,1,0:T(8,128)(2,1)} %collective-permute-done.1), kind=kLoop, calls=%fused_computation.415 | loop fusion | bytes 19660800
  697.1 8.5 %constant_dynamic-update-slice_fusion.1 = bf16[80,2,640,320]{3,2,1,0:T(8,128)(2,1)} fusion(bf16[80,2,640,320]{3,2,1,0:T(8,128)(2,1)} %constant_dynamic-update-slice_fusion.2, bf16[80,2,80,320]{3,2,1,0:T(8,128)(2,1)} %copy-done.2), kind=kLoop, calls=%fused_computation.414 | loop fusion | bytes 19660800
  705.6 8.5 %constant_dynamic-update-slice_fusion = bf16[80,2,640,320]{3,2,1,0:T(8,128)(2,1)} fusion(bf16[80,2,640,320]{3,2,1,0:T(8,128)(2,1)} %constant_dynamic-update-slice_fusion.1, bf16[80,2,80,320]{3,2,1,0:T(8,128)(2,1)} %param.12), kind=kLoop, calls=%fused_computation.413 | loop fusion | bytes 19660800 | tf_op jit(solution)/shard_map/jit(_roll_dynamic)/concatenate | solution.py:104
  714.1 17.4 %fusion.2 = f32[80,2,320,2,2]{2,4,3,1,0:T(2,128)S(1)} fusion(bf16[80,2,640,320]{3,2,1,0:T(8,128)(2,1)} %constant_dynamic-update-slice_fusion, s32[]{:T(128)S(6)} %select_n.55, bf16[80,1,2,2,320]{4,3,2,1,0:T(2,128)(2,1)S(1)} %fusion.203, bf16[80,1,2,2,320]{4,3,2,1,0:T(2,128)(2,1)S(1)} %get-tuple-element.2), kind=kOutput, calls=%fused_computation.2 | convolution fusion | flops 131891200 | bytes 40550404 | tf_op jit(solution)/shard_map/rpij,rpclj->rpicl/dot_general | solution.py:105
  731.5 2.0 copy.57
  733.6 3.5 all-to-all-start.1
  738.3 28.1 %all-to-all-done.1 = f32[80,2,320,2,2]{0,4,3,1,2:T(2,128)S(1)} async-done(((f32[80,2,320,2,2]{0,4,3,1,2:T(2,128)}), f32[80,2,320,2,2]{0,4,3,1,2:T(2,128)S(1)}, u32[]{:S(2)}, u32[]{:S(2)}) %all-to-all-start.1) | async-done | bytes 819232 | tf_op jit(solution)/shard_map/all_to_all | solution.py:108
  768.7 1.6 convolution_divide_fusion
  770.3 2.3 fusion.243
  773.1 19.5 %all_to_all.72 = bf16[80,2,80,2,8]{2,3,1,0,4:T(2,128)(2,1)S(1)} all-to-all(bf16[80,2,80,2,8]{2,3,1,0,4:T(2,128)(2,1)S(1)} %copy.62), channel_id=1, replica_groups=mesh['lat'=8,'lev'=4] {'lev'}, dimensions={4} | all-to-all | bytes 819200 | tf_op jit(solution)/shard_map/all_to_all | solution.py:111
  794.7 16.7 %fusion.23 = f32[2,80,2,2,320]{4,0,3,2,1:T(2,128)S(1)} fusion(bf16[80,2,320,2,2]{2,4,3,1,0:T(2,128)(2,1)S(1)} %all_to_all.63, bf16[80,2,640,320]{3,2,1,0:T(8,128)(2,1)} %constant_dynamic-update-slice_fusion, s32[]{:T(128)S(6)} %select_n.55), kind=kOutput, calls=%fused_computation.72 | convolution fusion | flops 131072000 | bytes 40550404 | tf_op jit(solution)/shard_map/rpij,rpicl->lrpcj/dot_general | solution.py:112
  812.0 1.5 reverse.2
  814.7 2.7 copy.67
  817.4 3.9 all-to-all-start.3
  821.3 16.1 %cosine_multiply_fusion = (f32[640,1,1280]{2,0,1:T(8,128)}, f32[640,1,1280]{2,0,1:T(8,128)}) fusion(f32[640]{0:T(1024)S(1)} %select_multiply_fusion, s32[640]{0:T(1024)S(1)} %copy-done.5), kind=kLoop, calls=%fused_computation.59 | loop fusion | flops 9830400 | bytes 6558720 | tf_op jit(solution)/shard_map/mul | solution.py:57
  837.3 2.0 all-to-all-done.3
  840.5 7.7 fusion.22
  (56 shorter events, 21.9 us)
Async XLA Ops:
  0.6 769.7 %copy-start = (f32[8,8]{1,0:T(8,128)S(1)}, f32[8,8]{1,0:T(8,128)}, u32[]{:S(2)}) copy-start(f32[8,8]{1,0:T(8,128)} %param.14) | copy-start | bytes 772
  0.6 237.3 %copy-start.3 = (s32[2,80,1280]{2,1,0:T(8,128)S(1)}, s32[2,80,1280]{2,1,0:T(8,128)}, u32[]{:S(2)}) copy-start(s32[2,80,1280]{2,1,0:T(8,128)} %param.9) | copy-start | bytes 2457604
  0.7 216.7 %collective-permute-start = (bf16[80,2,80,320]{3,2,1,0:T(8,128)(2,1)}, bf16[80,2,80,320]{3,2,1,0:T(8,128)(2,1)S(1)}, u32[]{:S(2)}, u32[]{:S(2)}) collective-permute-start(bf16[80,2,80,320]{3,2,1,0:T(8,128)(2,1)} %param.12), channel_id=1, source_target_pairs={{0,1},{1,2},{2,3},{3,0},{4,5},{5,6},{6,7},{7,4},{8,9},{9,10},{10,1... | collective-permute-start | bytes 24576008 | tf_op jit(solution)/shard_map/ppermute | solution.py:101
  217.4 45.8 %copy-start.2 = (bf16[80,2,80,320]{3,2,1,0:T(8,128)(2,1)}, bf16[80,2,80,320]{3,2,1,0:T(8,128)(2,1)S(1)}, u32[]{:S(2)}) copy-start(bf16[80,2,80,320]{3,2,1,0:T(8,128)(2,1)S(1)} %collective-permute-done) | copy-start | bytes 24576004
  217.4 214.4 %collective-permute-start.1 = (bf16[80,2,80,320]{3,2,1,0:T(8,128)(2,1)S(1)}, bf16[80,2,80,320]{3,2,1,0:T(8,128)(2,1)}, u32[]{:S(2)}, u32[]{:S(2)}) collective-permute-start(bf16[80,2,80,320]{3,2,1,0:T(8,128)(2,1)S(1)} %collective-permute-done), channel_id=1, source_target_pairs={{0,1},{1,2},{2,3},{3,0},{4,5},{5,6},{6,7},{7,4},{8,9},{9,10},{10,1... | collective-permute-start | bytes 24576008 | tf_op jit(solution)/shard_map/ppermute | solution.py:101
  218.5 67.9 %collective-permute-start.4 = (f32[2,3,1280]{2,1,0:T(4,128)S(1)}, f32[2,3,1280]{2,1,0:T(4,128)S(1)}, u32[]{:S(2)}, u32[]{:S(2)}) collective-permute-start(f32[2,3,1280]{2,1,0:T(4,128)S(1)} %get-tuple-element.141), channel_id=1, source_target_pairs={{4,0},{8,4},{12,8},{16,12},{20,16},{24,20},{28,24},{5,1},{9,5},{13... | collective-permute-start | bytes 92168 | tf_op jit(solution)/shard_map/ppermute | solution.py:21
  219.8 68.4 %collective-permute-start.3 = (f32[2,3,1280]{2,1,0:T(4,128)S(1)}, f32[2,3,1280]{2,1,0:T(4,128)S(1)}, u32[]{:S(2)}, u32[]{:S(2)}) collective-permute-start(f32[2,3,1280]{2,1,0:T(4,128)S(1)} %get-tuple-element.140), channel_id=1, source_target_pairs={{0,4},{4,8},{8,12},{12,16},{16,20},{20,24},{24,28},{1,5},{5,9},{9,... | collective-permute-start | bytes 92168 | tf_op jit(solution)/shard_map/ppermute | solution.py:19
  263.2 9.7 %copy-start.5 = (s32[640]{0:T(1024)S(1)}, s32[640]{0:T(1024)}, u32[]{:S(2)}) copy-start(s32[640]{0:T(1024)} %param.11) | copy-start | bytes 7684
  272.9 13.4 %copy-start.1 = (f32[2,80,1280]{2,1,0:T(8,128)S(1)}, f32[2,80,1280]{2,1,0:T(8,128)}, u32[]{:S(2)}) copy-start(f32[2,80,1280]{2,1,0:T(8,128)} %param.8) | copy-start | bytes 2457604
  431.8 214.1 %collective-permute-start.2 = (bf16[80,2,80,320]{3,2,1,0:T(8,128)(2,1)}, bf16[80,2,80,320]{3,2,1,0:T(8,128)(2,1)}, u32[]{:S(2)}, u32[]{:S(2)}) collective-permute-start(bf16[80,2,80,320]{3,2,1,0:T(8,128)(2,1)} %collective-permute-done.1), channel_id=1, source_target_pairs={{0,1},{1,2},{2,3},{3,0},{4,5},{5,6},{6,7},{7,4},{8,9},{9,10},{10,1... | collective-permute-start | bytes 24576008 | tf_op jit(solution)/shard_map/ppermute | solution.py:101
  485.4 21.9 %all-to-all-start = ((f32[640,2,2,80]{3,2,1,0:T(2,128)}), f32[640,2,2,80]{3,2,1,0:T(2,128)S(1)}, u32[]{:S(2)}, u32[]{:S(2)}) async-start(f32[640,2,2,80]{3,2,1,0:T(2,128)} %copy.54), calls=%async_computation | async-start | bytes 2621440 | tf_op jit(solution)/shard_map/all_to_all | solution.py:93
  731.5 5.9 copy-start.6
  733.6 32.8 %all-to-all-start.1 = ((f32[80,2,320,2,2]{0,4,3,1,2:T(2,128)}), f32[80,2,320,2,2]{0,4,3,1,2:T(2,128)S(1)}, u32[]{:S(2)}, u32[]{:S(2)}) async-start(f32[80,2,320,2,2]{0,4,3,1,2:T(2,128)} %copy.57), calls=%async_computation.1 | async-start | bytes 2621440 | tf_op jit(solution)/shard_map/all_to_all | solution.py:108
  767.6 1.1 copy-start.4
  767.6 1.1 copy-start.7
  817.4 22.0 %all-to-all-start.3 = ((f32[2,80,2,640]{1,2,0,3:T(2,128)}), f32[2,80,2,640]{1,2,0,3:T(2,128)S(1)}, u32[]{:S(2)}, u32[]{:S(2)}) async-start(f32[2,80,2,640]{1,2,0,3:T(2,128)} %copy.67), calls=%async_computation.3 | async-start | bytes 2621440 | tf_op jit(solution)/shard_map/all_to_all | solution.py:118
